TPU v7x, 512 devices: a whole 4x4x16 slice. The times are simulated.
512 devices in a mesh: dp: 8 (over z_hi, x), row: 8 (over y, core), col: 8 (over z_lo).
Axes of the slice: x: 4, y: 4, z: 16 (z_hi: 2, z_lo: 8; z = z_hi * 8 + z_lo), core: 2. Of those that a mesh axis runs over, the one named last changes fastest.
Arguments:
- tokens: bfloat16 [65536, 8192], P(('dp', 'row', 'col')), parts along dimension 0, may hold values from -60 to 60
- norm_gain: float32 [8192], replicated, may hold values from 0.1 to 1.9
- w_key: bfloat16 [8192, 1024], P('row', 'col'), may hold values from -0.0625 to 0.0625
- w_value: bfloat16 [8192, 1024], P('row', 'col'), may hold values from -0.0625 to 0.0625
Outputs:
- key_rows: bfloat16 [65536, 1024], P(('dp', 'row', 'col')), parts along dimension 0
- value_rows: bfloat16 [65536, 1024], P(('dp', 'row', 'col')), parts along dimension 0
There are 8 independent parts, one for each index of `dp`. A program takes and returns all parts, laid end to end along the dimension named above; an argument that names none is the same for every part. Nothing has to cross between parts.
All inputs are finite; a program needn't handle non-finite values.
Results may differ from a plain program's by a relative error of at most 0.014.
Values may be sent and summed in bfloat16 or wider, within the bound.
A program may use at most 64 MiB of HBM per device.

v0:
```python
import jax
import jax.numpy as jnp
from jax import lax
from jax.sharding import PartitionSpec as P

HEAD = 128


rope_base = 500000.0


def rotate(projected, positions):
    row_count = projected.shape[0]
    head_count = projected.shape[1] // HEAD
    half_head = HEAD // 2
    frequency = rope_base ** (-2.0 * jnp.arange(half_head, dtype=jnp.float32) / HEAD)
    angles = positions.astype(jnp.float32)[:, None] * frequency[None, :]
    cosine = jnp.cos(angles)[:, None, :]
    sine = jnp.sin(angles)[:, None, :]
    split_heads = projected.reshape(row_count, head_count, HEAD)
    first = split_heads[:, :, :half_head]
    second = split_heads[:, :, half_head:]
    turned = jnp.concatenate(
        [first * cosine - second * sine, second * cosine + first * sine], axis=2
    )
    return turned.reshape(row_count, head_count * HEAD)


def body(tokens, norm_gain, w_key, w_value):
    col_count = lax.axis_size("col")
    row_index = lax.axis_index("row")
    col_index = lax.axis_index("col")
    own_rows = tokens.shape[0]
    widened = tokens.astype(jnp.float32)
    inverse_rms = lax.rsqrt(jnp.mean(widened * widened, axis=1, keepdims=True) + 1e-05)
    normed = (widened * inverse_rms * norm_gain[None, :]).astype(jnp.bfloat16)
    tile = lax.all_to_all(normed, "row", split_axis=1, concat_axis=0, tiled=True)
    key_weights, value_weights = (
        lax.all_gather(w_key, "col", axis=1, tiled=True),
        lax.all_gather(w_value, "col", axis=1, tiled=True),
    )
    key_part = jnp.dot(tile, key_weights, preferred_element_type=jnp.float32)
    value_part = jnp.dot(tile, value_weights, preferred_element_type=jnp.float32)
    key_sum, value_sum = (
        lax.psum_scatter(
            key_part.astype(jnp.bfloat16), "row", scatter_dimension=0, tiled=True
        ).astype(jnp.float32),
        lax.psum_scatter(
            value_part.astype(jnp.bfloat16), "row", scatter_dimension=0, tiled=True
        ).astype(jnp.float32),
    )
    positions = (row_index * col_count + col_index) * own_rows + jnp.arange(
        own_rows, dtype=jnp.int32
    )
    key_rows = rotate(key_sum, positions).astype(jnp.bfloat16)
    value_rows = value_sum.astype(jnp.bfloat16)
    return (key_rows, value_rows)


def solution(mesh):
    placed = (P(("dp", "row", "col"), None), P(), P("row", "col"), P("row", "col"))
    return jax.shard_map(
        body,
        mesh=mesh,
        in_specs=placed,
        out_specs=(P(("dp", "row", "col"), None), P(("dp", "row", "col"), None)),
        check_vma=False,
    )
```

profile of v0, /device:TPU:1, one launch (start us, length us, event | category | flops | bytes accessed | tf_op | source)
XLA Modules:
  0.0 247.8 jit_solution(14497560311085529130)
XLA Ops:
  7.2 0.0 all-gather.3.cloned.1.call-start
  7.2 0.7 all-gather.3.cloned.1.call-update
  7.9 0.0 all-gather.5.cloned.1.call-start
  7.9 0.7 all-gather.5.cloned.1.call-update
  8.6 0.0 reduce-scatter.3.cloned.1.call-start
  8.7 3.2 %copy.6 = bf16[128,8192]{0,1:T(8,128)(2,1)S(1)} copy(bf16[128,8192]{1,0:T(8,128)(2,1)} %param.4) | data formatting | bytes 4194304 | tf_op args[0]
  11.9 0.0 copy-start.1
  11.9 1.1 fusion
  13.0 0.0 copy-done.1
  13.0 3.5 %fusion.2 = bf16[128,8192]{0,1:T(8,128)(2,1)S(1)} fusion(bf16[128,8192]{0,1:T(8,128)(2,1)S(1)} %copy.6, f32[8192]{0:T(1024)S(1)} %copy-done.1, f32[128]{0:T(128)S(1)} %add_rsqrt_fusion), kind=kLoop, calls=%fused_computation.4 | loop fusion | flops 4194304 | bytes 4227584 | tf_op jit(solution)/shard_map/convert_element_type | solution.py:36
  16.5 35.8 %all_to_all.19 = bf16[128,8,1024]{0,2,1:T(8,128)(2,1)S(1)} all-to-all(bf16[128,8,1024]{0,2,1:T(8,128)(2,1)S(1)} %bitcast.14), channel_id=1, replica_groups=mesh['dp'=8,'row'=8,'col'=8] {'row'}, dimensions={1} | all-to-all | bytes 4194304 | tf_op jit(solution)/shard_map/all_to_all | solution.py:37
  52.3 2.6 %copy.7 = bf16[8,128,1024]{2,1,0:T(8,128)(2,1)} copy(bf16[8,128,1024]{1,2,0:T(8,128)(2,1)S(1)} %bitcast.15) | data formatting | bytes 4194304 | tf_op jit(solution)/shard_map/all_to_all | solution.py:37
  55.0 27.6 %all-gather.3.cloned.1.call-done = bf16[1024,1024]{1,0:T(8,128)(2,1)} async-done(((bf16[1024,128]{1,0:T(8,128)(2,1)}), bf16[1024,1024]{1,0:T(8,128)(2,1)}) %all-gather.3.cloned.1.call-update) | async-done | bytes 2097168 | tf_op jit(solution)/shard_map/all_gather | solution.py:39
  82.5 5.9 %convolution_convert_fusion.1 = bf16[1024,1024]{1,0:T(8,128)(2,1)} fusion(bf16[1024,1024]{1,0:T(8,128)(2,1)} %bitcast.17, bf16[1024,1024]{1,0:T(8,128)(2,1)} %all-gather.3.cloned.1.call-done), kind=kOutput, calls=%fused_computation.6 | convolution fusion | flops 2148532224 | bytes 6291456 | tf_op jit(solution)/shard_map/dot_general | solution.py:42
  88.4 0.0 copy-start
  88.4 0.0 reduce-scatter.3.cloned.1.call-update
  88.4 0.0 reduce-scatter.5.cloned.1.call-start
  88.4 65.2 %all-gather.5.cloned.1.call-done = bf16[1024,1024]{1,0:T(8,128)(2,1)} async-done(((bf16[1024,128]{1,0:T(8,128)(2,1)}), bf16[1024,1024]{1,0:T(8,128)(2,1)}) %all-gather.5.cloned.1.call-update) | async-done | bytes 2097168 | tf_op jit(solution)/shard_map/all_gather | solution.py:40
  153.6 0.0 copy-done
  153.6 5.3 %convolution_convert_fusion = bf16[1024,1024]{1,0:T(8,128)(2,1)} fusion(bf16[1024,1024]{1,0:T(8,128)(2,1)S(1)} %bitcast.18, bf16[1024,1024]{1,0:T(8,128)(2,1)} %all-gather.5.cloned.1.call-done), kind=kOutput, calls=%fused_computation.5 | convolution fusion | flops 2148532224 | bytes 6291456 | tf_op jit(solution)/shard_map/dot_general | solution.py:43
  158.9 0.0 reduce-scatter.5.cloned.1.call-update
  158.9 0.3 multiply_cosine_fusion
  159.3 38.5 %reduce-scatter.3.cloned.1.call-done = bf16[128,1024]{1,0:T(8,128)(2,1)} async-done(((bf16[1024,1024]{1,0:T(8,128)(2,1)}), bf16[128,1024]{1,0:T(8,128)(2,1)}) %reduce-scatter.3.cloned.1.call-update) | async-done | bytes 262160 | tf_op jit(solution)/shard_map/reduce_scatter | solution.py:45
  197.8 1.0 convert_bitcast_fusion
  198.8 0.1 copy.8
  198.9 0.3 subtract_convert_fusion
  199.2 0.1 pad_maximum_fusion
  199.3 0.8 copy.11
  200.1 41.2 %reduce-scatter.5.cloned.1.call-done = bf16[128,1024]{1,0:T(8,128)(2,1)} async-done(((bf16[1024,1024]{1,0:T(8,128)(2,1)}), bf16[128,1024]{1,0:T(8,128)(2,1)}) %reduce-scatter.5.cloned.1.call-update) | async-done | bytes 262160 | tf_op jit(solution)/shard_map/reduce_scatter | solution.py:48
  (3 shorter events, 0.0 us)
Async XLA Ops:
  7.2 75.3 %all-gather.3.cloned.1.call-start = ((), (), s32[]{:S(2)}) async-start(), calls=%async_computation.3 | async-start | bytes 2359296 | tf_op jit(solution)/shard_map/all_gather | solution.py:39
  7.9 145.7 %all-gather.5.cloned.1.call-start = ((), (), s32[]{:S(2)}) async-start(), calls=%async_computation.5 | async-start | bytes 2359296 | tf_op jit(solution)/shard_map/all_gather | solution.py:40
  8.6 189.1 %reduce-scatter.3.cloned.1.call-start = ((), (), s32[]{:S(2)}) async-start(), calls=%async_computation.4 | async-start | bytes 2359296 | tf_op jit(solution)/shard_map/reduce_scatter | solution.py:45
  11.9 1.1 copy-start.1
  88.4 65.3 %copy-start = (bf16[8,128,1024]{2,1,0:T(8,128)(2,1)S(1)}, bf16[8,128,1024]{2,1,0:T(8,128)(2,1)}, u32[]{:S(2)}) copy-start(bf16[8,128,1024]{2,1,0:T(8,128)(2,1)} %copy.7) | copy-start | bytes 6291460
  88.4 152.9 %reduce-scatter.5.cloned.1.call-start = ((), (), s32[]{:S(2)}) async-start(), calls=%async_computation.6 | async-start | bytes 2359296 | tf_op jit(solution)/shard_map/reduce_scatter | solution.py:48
Sparse Core Ops, SparseCore 0:
  10.0 72.4 all-gather.2
  84.5 69.0 all-gather.4
  156.5 41.2 reduce-scatter.2
  201.1 40.1 reduce-scatter.4
where the time goes:
time: 249 us; the launch traced here: 248 us
  waiting for transfers between devices  174 us (70%)
  blocking collectives  35.8 us (14%)
  between operations  13.8 us (6%)
  matrix products  11.1 us (4%)
  local copies, waits for them, and re-layouts  6.71 us (3%)
  other arithmetic  6.31 us (3%)
    all_gather x1, waiting for transfers between devices, body(): lax.all_gather(w_value, 'col', axis=1, tiled=True)  65.2 us
    reduce_scatter x1, waiting for transfers between devices, body(): lax.psum_scatter(value_part.astype(jnp.bfloat16), 'row', scatter_dimensio...  41.2 us
    reduce_scatter x1, waiting for transfers between devices, body(): lax.psum_scatter(key_part.astype(jnp.bfloat16), 'row', scatter_dimension=...  38.5 us
    all_to_all x1, blocking collectives, body(): lax.all_to_all(normed, 'row', split_axis=1, concat_axis=0, tiled=True)  35.8 us
    all_gather x1, waiting for transfers between devices, body(): lax.all_gather(w_key, 'col', axis=1, tiled=True)  27.6 us
    dot_general x1, matrix products, body(): key_part = jnp.dot(tile, key_weights, preferred_element_type=jnp.float32)  5.86 us
    dot_general x1, matrix products, body(): jnp.dot(tile, value_weights, preferred_element_type=jnp.float32)  5.26 us
  transfers between devices with their start and end apart: 4, of which 4 were waited for; matrix products, arithmetic and copies ran while one was open for 10% of the time, Pallas kernels for 0%

commit v1 on v0

v1 whole, which is shorter than its diff:
```python
import functools

import jax
import jax.numpy as jnp
from jax import lax
from jax.experimental import pallas as pl
from jax.experimental.pallas import tpu as pltpu
from jax.sharding import PartitionSpec as P

HEAD = 128
EPS = 1e-05
MESH = pl.DeviceIdType.MESH

rope_base = 500000.0

UNITS = (0, 1, 7, 2, 6, 3, 5, 4)


def rotation_tables(positions):
    half_head = HEAD // 2
    frequency = rope_base ** (-2.0 * jnp.arange(half_head, dtype=jnp.float32) / HEAD)
    angles = positions.astype(jnp.float32)[:, None] * frequency[None, :]
    cosine = jnp.cos(angles)
    sine = jnp.sin(angles)
    return (
        jnp.concatenate([cosine, cosine], axis=1),
        jnp.concatenate([-sine, sine], axis=1),
    )


def kernel(
    tokens, gain, w_key, w_value, cosine, sine, key_out, value_out,
    tok, tile, weights, hop, kept, pair_out, pair_in, far_out, far_in, near_out, near_in, scale,
    local_sem, z_send, z_recv, hop_send, hop_recv, tile_send, tile_recv,
    pair_send, pair_recv, far_send, far_recv, near_send, near_recv,
):
    rows = tokens.shape[0]
    depth, width = w_key.shape
    half = rows // 2
    dp, row, col = lax.axis_index("dp"), lax.axis_index("row"), lax.axis_index("col")
    y, core = row // 2, row % 2
    other = 1 - core

    def at(step, which):
        return (dp, ((y + step + 4) % 4) * 2 + which, col)

    wrap_up, wrap_down = col // 7, (7 - col) // 7
    z_next = ((dp + 4 * wrap_up) % 8, row, (col + 1) % 8)
    z_prev = ((dp + 4 * wrap_down) % 8, row, (col + 7) % 8)

    partners = [at(1, core), at(3, core), at(1, other), at(3, other), at(0, other), z_next, z_prev]
    barrier = pltpu.get_barrier_semaphore()
    for partner in partners:
        pl.semaphore_signal(barrier, inc=1, device_id=partner, device_id_type=MESH)
    pl.semaphore_wait(barrier, len(partners))

    sent = []

    def remote(src, dst, send, recv, device):
        return pltpu.make_async_remote_copy(
            src_ref=src, dst_ref=dst, send_sem=send, recv_sem=recv, device_id=device, device_id_type=MESH
        )

    def go(copy):
        copy.start()
        sent.append(copy)
        return copy

    def features(step, which):
        index = ((y + step) % 4) * 2 + which
        return tokens.at[:, pl.ds(pl.multiple_of(index * depth, depth), depth)]

    def tile_rows(kind, step):
        return tile.at[pl.ds((kind * 4 + step) * rows, rows), :]

    def piece(way, j):
        distance = j // 2 + 1
        kind = (j + way) % 2
        columns = pl.ds(kind * width, width)
        to = distance if way == 0 else 8 - distance
        back = (distance - 1) if way == 0 else (9 - distance) % 8
        src = (w_key, w_value)[kind] if distance == 1 else weights.at[back, :, columns]
        return remote(
            src, weights.at[to, :, columns], z_send.at[way, j], z_recv.at[way, j], (z_next, z_prev)[way]
        )

    pieces = [[piece(way, j) for j in range(7)] for way in range(2)]
    for j in range(2):
        for way in range(2):
            go(pieces[way][j])
    hops = [
        go(remote(features(2, core), hop.at[0], hop_send.at[0], hop_recv.at[0], at(1, core))),
        go(remote(features(2, other), hop.at[1], hop_send.at[1], hop_recv.at[1], at(3, core))),
    ]
    blocks = {}
    for kind, step in ((0, 1), (0, 3), (1, 1), (1, 3), (1, 0)):
        which = other if kind else core
        slot = (4 - step) % 4
        blocks[kind, slot] = go(
            remote(features(step, which), tile_rows(kind, slot), tile_send.at[kind, slot], tile_recv.at[kind, slot], at(step, which))
        )
    own_tile = pltpu.make_async_copy(features(0, core), tile_rows(0, 0), local_sem.at[0])
    own_key = pltpu.make_async_copy(w_key, weights.at[0, :, pl.ds(0, width)], local_sem.at[1])
    own_value = pltpu.make_async_copy(w_value, weights.at[0, :, pl.ds(width, width)], local_sem.at[2])
    own_tokens = pltpu.make_async_copy(tokens, tok, local_sem.at[3])
    for copy in (own_tokens, own_tile, own_key, own_value):
        copy.start()

    own_tokens.wait()

    def squares(i, total):
        part = tok[:, pl.ds(pl.multiple_of(i * 128, 128), 128)].astype(jnp.float32)
        return total + part * part

    total = lax.fori_loop(0, tokens.shape[1] // 128, squares, jnp.zeros((rows, 128), jnp.float32))
    mean = jnp.sum(total, axis=1, keepdims=True) / tokens.shape[1]
    scale[...] = jnp.broadcast_to(lax.rsqrt(mean + EPS), scale.shape)

    own_gain = gain[:, pl.ds(pl.multiple_of(row * depth, depth), depth)]

    def weigh(kind, step):
        ref = tile_rows(kind, step)
        ref[...] = (ref[...].astype(jnp.float32) * own_gain).astype(jnp.bfloat16)

    def arrive(j):
        for way in range(2):
            pieces[way][j].wait_recv()
            if j + 2 < 7:
                go(pieces[way][j + 2])

    arrive(0)
    hops[0].wait_recv()
    blocks[0, 2] = go(remote(hop.at[0], tile_rows(0, 2), tile_send.at[0, 2], tile_recv.at[0, 2], at(1, core)))
    hops[1].wait_recv()
    blocks[1, 2] = go(remote(hop.at[1], tile_rows(1, 2), tile_send.at[1, 2], tile_recv.at[1, 2], at(3, other)))
    own_tile.wait()
    weigh(0, 0)
    blocks[1, 0].wait_recv()
    weigh(1, 0)
    arrive(1)
    for slot in (1, 3):
        blocks[0, slot].wait_recv()
        weigh(0, slot)
    arrive(2)
    for slot in (1, 3):
        blocks[1, slot].wait_recv()
        weigh(1, slot)
    arrive(3)
    for kind in (1, 0):
        blocks[kind, 2].wait_recv()
        weigh(kind, 2)
    own_key.wait()
    own_value.wait()

    pairs, fars, nears = {}, {}, {}

    def multiply(u):
        w = weights[UNITS[u]]
        pair_out[u] = jnp.dot(
            tile[pl.ds(4 * rows, 4 * rows), :], w, preferred_element_type=jnp.float32
        ).astype(jnp.bfloat16)
        pairs[u] = go(remote(pair_out.at[u], pair_in.at[u], pair_send.at[u], pair_recv.at[u], at(0, other)))
        kept[u] = jnp.dot(tile[pl.ds(0, 4 * rows), :], w, preferred_element_type=jnp.float32)

    def chip_sum(u, step, low, size):
        at_rows = pl.ds(step * rows + low, size)
        return kept[u, at_rows, :] + pair_in[u, at_rows, :].astype(jnp.float32)

    def relay(u):
        pairs[u].wait_recv()
        for way in range(2):
            far_out[u, way] = chip_sum(u, 2, way * half, half).astype(jnp.bfloat16)
            fars[u, way] = go(
                remote(far_out.at[u, way], far_in.at[u, way], far_send.at[u, way], far_recv.at[u, way], at((1, 3)[way], core))
            )

    def neighbour(u):
        for way in range(2):
            step = (1, 3)[way]
            fars[u, way].wait_recv()
            mine, through = pl.ds((1 - way) * half, half), pl.ds(way * half, half)
            near_out[u, way, mine, :] = chip_sum(u, step, (1 - way) * half, half).astype(jnp.bfloat16)
            near_out[u, way, through, :] = (
                chip_sum(u, step, way * half, half) + far_in[u, way].astype(jnp.float32)
            ).astype(jnp.bfloat16)
            nears[u, way] = go(
                remote(near_out.at[u, way], near_in.at[u, way], near_send.at[u, way], near_recv.at[u, way], at(step, core))
            )

    def finish(u):
        result = chip_sum(u, 0, 0, rows)
        for way in range(2):
            nears[u, way].wait_recv()
            result = result + near_in[u, way].astype(jnp.float32)
        key, value = result[:, :width] * scale[...], result[:, width:] * scale[...]
        turned = key * cosine[...] + pltpu.roll(key, HEAD // 2, 1) * sine[...]
        columns = pl.ds(pl.multiple_of(((col + 8 - UNITS[u]) % 8) * width, width), width)
        key_out[:, columns] = turned.astype(jnp.bfloat16)
        value_out[:, columns] = value.astype(jnp.bfloat16)

    count = len(UNITS)
    for step in range(count + 3):
        if step == 5:
            arrive(5)
        if step == 7:
            arrive(6)
        if step < count:
            multiply(step)
        if step == 2:
            arrive(4)
        if 0 <= step - 1 < count:
            relay(step - 1)
        if 0 <= step - 2 < count:
            neighbour(step - 2)
        if 0 <= step - 3 < count:
            finish(step - 3)
    for copy in sent:
        copy.wait_send()


def body(tokens, norm_gain, w_key, w_value):
    rows, model = tokens.shape
    depth, width = w_key.shape
    pair = 2 * width
    first = (lax.axis_index("row") * lax.axis_size("col") + lax.axis_index("col")) * rows
    cosine, sine = rotation_tables(first + jnp.arange(rows, dtype=jnp.int32))
    units = len(UNITS)
    bf16, f32 = jnp.bfloat16, jnp.float32
    dma = pltpu.SemaphoreType.DMA
    anywhere = pl.BlockSpec(memory_space=pl.ANY)
    vmem = pl.BlockSpec(memory_space=pltpu.VMEM)
    out = jax.ShapeDtypeStruct((rows, units * width), bf16)
    return pl.pallas_call(
        kernel,
        name="key_value",
        out_shape=(out, out),
        in_specs=[anywhere, vmem, anywhere, anywhere, vmem, vmem],
        out_specs=(vmem, vmem),
        scratch_shapes=[
            pltpu.VMEM((rows, model), bf16),
            pltpu.VMEM((8 * rows, depth), bf16),
            pltpu.VMEM((units, depth, pair), bf16),
            pltpu.VMEM((2, rows, depth), bf16),
            pltpu.VMEM((units, 4 * rows, pair), f32),
            pltpu.VMEM((units, 4 * rows, pair), bf16),
            pltpu.VMEM((units, 4 * rows, pair), bf16),
            pltpu.VMEM((units, 2, rows // 2, pair), bf16),
            pltpu.VMEM((units, 2, rows // 2, pair), bf16),
            pltpu.VMEM((units, 2, rows, pair), bf16),
            pltpu.VMEM((units, 2, rows, pair), bf16),
            pltpu.VMEM((rows, width), f32),
            dma((4,)),
            dma((2, 7)), dma((2, 7)),
            dma((2,)), dma((2,)),
            dma((2, 4)), dma((2, 4)),
            dma((units,)), dma((units,)),
            dma((units, 2)), dma((units, 2)),
            dma((units, 2)), dma((units, 2)),
        ],
        compiler_params=pltpu.CompilerParams(collective_id=0, has_side_effects=True),
    )(tokens, norm_gain.reshape(1, model), w_key, w_value, cosine, sine)


def solution(mesh):
    placed = (P(("dp", "row", "col"), None), P(), P("row", "col"), P("row", "col"))
    return jax.shard_map(
        body,
        mesh=mesh,
        in_specs=placed,
        out_specs=(P(("dp", "row", "col"), None), P(("dp", "row", "col"), None)),
        check_vma=False,
    )
```

time: 249 us -> 76.1 us (0.31)
  waiting for transfers between devices: 174 us -> 0 us
  Pallas kernels: 0 us -> 69.8 us
  blocking collectives: 35.8 us -> 0 us
  between operations: 13.8 us -> 0.66 us
  matrix products: 11.1 us -> 0 us
  other arithmetic: 6.31 us -> 1.08 us
  local copies, waits for them, and re-layouts: 6.71 us -> 3.34 us
    all_gather x2 -> x0, waiting for transfers between devices: 92.7 us -> none  [the longest x1 65.2 us: body(): lax.all_gather(w_value, 'col', axis=1, tiled=True)]
    reduce_scatter x2 -> x0, waiting for transfers between devices: 79.7 us -> none  [the longest x1 41.2 us: body(): lax.psum_scatter(value_part.astype(jnp.bfloat16), 'row', scatter_dimensio...]
    pallas_call x0 -> x1, Pallas kernels: none -> 69.8 us  [body(): pl.pallas_call(kernel, name='key_value', out_shape=(out, out), in_specs=[...]
    all_to_all x1 -> x0, blocking collectives: 35.8 us -> none  [body(): lax.all_to_all(normed, 'row', split_axis=1, concat_axis=0, tiled=True)]
    dot_general x2 -> x0, matrix products: 11.1 us -> none  [the longest x1 5.86 us: body(): key_part = jnp.dot(tile, key_weights, preferred_element_type=jnp.float32)]
    convert_element_type x2 -> x1, other arithmetic: 3.49 us -> 0.01 us  [rotation_tables(): angles = positions.astype(jnp.float32)[:, None] * frequency[None, :]]
    all_to_all x1 -> x0, local copies, waits for them, and re-layouts: 2.63 us -> none  [body(): lax.all_to_all(normed, 'row', split_axis=1, concat_axis=0, tiled=True)]
  transfers between devices with their start and end apart: 4 -> 0, of which waited for: 4 -> 0; matrix products, arithmetic and copies ran while one was open for 10% -> 0% of each run, Pallas kernels for 0% -> 0%
where the time goes in v1:
time: 76.1 us; the launch traced here: 74.8 us
  Pallas kernels  69.8 us (92%)
  local copies, waits for them, and re-layouts  3.34 us (4%)
  other arithmetic  1.08 us (1%)
    pallas_call x1, Pallas kernels, body(): pl.pallas_call(kernel, name='key_value', out_shape=(out, out), in_specs=[...  69.8 us
    unnamed x2, local copies, waits for them, and re-layouts  3.34 us

profile of v1, /device:TPU:1, one launch (start us, length us, event | category | flops | bytes accessed | tf_op | source)
XLA Modules:
  0.0 74.8 jit_solution(9325026947846361469)
XLA Ops:
  0.7 0.3 fusion
  1.0 0.8 %pad_maximum_fusion = (f32[128,128]{1,0:T(8,128)}, f32[128,128]{1,0:T(8,128)}) fusion(f32[128,64]{1,0:T(8,128)S(1)} %get-tuple-element.4, f32[128,64]{1,0:T(8,128)S(1)} %get-tuple-element.3, f32[128,64]{1,0:T(8,128)S(1)} %get-tuple-element.2), kind=kLoop, calls=%fused_computation.2 | loop fusion | flops 32768 | bytes 229376 | tf_op jit(solution)/shard_map/concatenate | solution.py:26
  1.7 69.8 %key_value.1 = (bf16[128,1024]{1,0:T(8,128)(2,1)}, bf16[128,1024]{1,0:T(8,128)(2,1)}) custom-call(bf16[128,8192]{1,0:T(8,128)(2,1)} %tokens.1, f32[1,8192]{1,0:T(1,128)} %bitcast.1, bf16[1024,128]{1,0:T(8,128)(2,1)} %w_key.1, bf16[1024,128]{1,0:T(8,128)(2,1)} %w_value.1, f32[128,128]{1,0:T(8,128)} %get-tuple-element.5.cosine, f32[128,128]{1,0:T(8,128)} %get-tuple-element.6.sine), custom_call_target="tpu_custom_call" | custom-call | tf_op jit(solution)/shard_map/key_value/pallas_call | solution.py:233
  71.5 1.7 %copy.8 = bf16[128,1024]{1,0:T(8,128)(2,1)} copy(bf16[128,1024]{1,0:T(8,128)(2,1)} %get-tuple-element.9) | data formatting | bytes 524288
  73.2 1.7 %copy.9 = bf16[128,1024]{1,0:T(8,128)(2,1)} copy(bf16[128,1024]{1,0:T(8,128)(2,1)} %get-tuple-element.10) | data formatting | bytes 524288
  (2 shorter events, 0.0 us)

commit v2 on v1

--- a/solution.py
+++ b/solution.py
@@ -1,7 +1,6 @@
-import functools
-
 import jax
 import jax.numpy as jnp
+import numpy as np
 from jax import lax
 from jax.experimental import pallas as pl
 from jax.experimental.pallas import tpu as pltpu
@@ -16,22 +15,18 @@
 UNITS = (0, 1, 7, 2, 6, 3, 5, 4)
 
 
-def rotation_tables(positions):
-    half_head = HEAD // 2
-    frequency = rope_base ** (-2.0 * jnp.arange(half_head, dtype=jnp.float32) / HEAD)
-    angles = positions.astype(jnp.float32)[:, None] * frequency[None, :]
-    cosine = jnp.cos(angles)
+def rotation_tables(first, frequency, shape):
+    lane = lax.broadcasted_iota(jnp.int32, shape, 1)
+    position = first + lax.broadcasted_iota(jnp.int32, shape, 0)
+    angles = position.astype(jnp.float32) * frequency
     sine = jnp.sin(angles)
-    return (
-        jnp.concatenate([cosine, cosine], axis=1),
-        jnp.concatenate([-sine, sine], axis=1),
-    )
+    return jnp.cos(angles), jnp.where(lane < HEAD // 2, -sine, sine)
 
 
 def kernel(
-    tokens, gain, w_key, w_value, cosine, sine, key_out, value_out,
-    tok, tile, weights, hop, kept, pair_out, pair_in, far_out, far_in, near_out, near_in, scale,
-    local_sem, z_send, z_recv, hop_send, hop_recv, tile_send, tile_recv,
+    tokens, gain, w_key, w_value, frequency, key_out, value_out,
+    tok, tile, weights, hop, kept, pair_out, pair_in, far_out, far_in, near_out, near_in, scale, cosine, sine,
+    local_sem, z_send, z_recv, x_send, x_recv, hop_send, hop_recv, tile_send, tile_recv,
     pair_send, pair_recv, far_send, far_recv, near_send, near_recv,
 ):
     rows = tokens.shape[0]
@@ -48,7 +43,25 @@
     z_next = ((dp + 4 * wrap_up) % 8, row, (col + 1) % 8)
     z_prev = ((dp + 4 * wrap_down) % 8, row, (col + 7) % 8)
 
-    partners = [at(1, core), at(3, core), at(1, other), at(3, other), at(0, other), z_next, z_prev]
+    x, kind_here = dp % 4, dp % 2
+    x_next = (dp - x + (x + 1) % 4, row, col)
+    x_prev = (dp - x + (x + 3) % 4, row, col)
+
+    partners = [at(1, core), at(3, core), at(1, other), at(3, other), at(0, other), z_next, z_prev, x_next, x_prev]
+    def features(step, which):
+        index = ((y + step) % 4) * 2 + which
+        return tokens.at[:, pl.ds(pl.multiple_of(index * depth, depth), depth)]
+
+    def tile_rows(kind, step):
+        return tile.at[pl.ds((kind * 4 + step) * rows, rows), :]
+
+    own_key = pltpu.make_async_copy(w_key, weights.at[0, :, pl.ds(0, width)], local_sem.at[1])
+    own_value = pltpu.make_async_copy(w_value, weights.at[0, :, pl.ds(width, width)], local_sem.at[2])
+    own_tile = pltpu.make_async_copy(features(0, core), tile_rows(0, 0), local_sem.at[0])
+    own_tokens = pltpu.make_async_copy(tokens, tok, local_sem.at[3])
+    for copy in (own_key, own_value, own_tile, own_tokens):
+        copy.start()
+
     barrier = pltpu.get_barrier_semaphore()
     for partner in partners:
         pl.semaphore_signal(barrier, inc=1, device_id=partner, device_id_type=MESH)
@@ -66,24 +79,28 @@
         sent.append(copy)
         return copy
 
-    def features(step, which):
-        index = ((y + step) % 4) * 2 + which
-        return tokens.at[:, pl.ds(pl.multiple_of(index * depth, depth), depth)]
-
-    def tile_rows(kind, step):
-        return tile.at[pl.ds((kind * 4 + step) * rows, rows), :]
+    def columns_of(kind):
+        return pl.ds(pl.multiple_of(kind * width, width), width)
+
+    def part(slot, j, way, kind):
+        return weights.at[slot, pl.ds(((j + way) % 2) * (depth // 2), depth // 2), columns_of(kind)]
+
+    def slot_of(way, distance):
+        return distance if way == 0 else (8 - distance) % 8
 
     def piece(way, j):
         distance = j // 2 + 1
-        kind = (j + way) % 2
-        columns = pl.ds(kind * width, width)
-        to = distance if way == 0 else 8 - distance
-        back = (distance - 1) if way == 0 else (9 - distance) % 8
-        src = (w_key, w_value)[kind] if distance == 1 else weights.at[back, :, columns]
         return remote(
-            src, weights.at[to, :, columns], z_send.at[way, j], z_recv.at[way, j], (z_next, z_prev)[way]
+            part(slot_of(way, distance - 1), j, way, kind_here), part(slot_of(way, distance), j, way, kind_here),
+            z_send.at[way, j], z_recv.at[way, j], (z_next, z_prev)[way],
         )
 
+    def across(way, j, kind):
+        block = part(slot_of(way, j // 2 + 1), j, way, kind)
+        return remote(block, block, x_send.at[way, j], x_recv.at[way, j], (x_next, x_prev)[(j + way) % 2])
+
+    own_key.wait()
+    own_value.wait()
     pieces = [[piece(way, j) for j in range(7)] for way in range(2)]
     for j in range(2):
         for way in range(2):
@@ -99,12 +116,6 @@
         blocks[kind, slot] = go(
             remote(features(step, which), tile_rows(kind, slot), tile_send.at[kind, slot], tile_recv.at[kind, slot], at(step, which))
         )
-    own_tile = pltpu.make_async_copy(features(0, core), tile_rows(0, 0), local_sem.at[0])
-    own_key = pltpu.make_async_copy(w_key, weights.at[0, :, pl.ds(0, width)], local_sem.at[1])
-    own_value = pltpu.make_async_copy(w_value, weights.at[0, :, pl.ds(width, width)], local_sem.at[2])
-    own_tokens = pltpu.make_async_copy(tokens, tok, local_sem.at[3])
-    for copy in (own_tokens, own_tile, own_key, own_value):
-        copy.start()
 
     own_tokens.wait()
 
@@ -116,6 +127,9 @@
     mean = jnp.sum(total, axis=1, keepdims=True) / tokens.shape[1]
     scale[...] = jnp.broadcast_to(lax.rsqrt(mean + EPS), scale.shape)
 
+    first = (row * 8 + col) * rows
+    cosine[...], sine[...] = rotation_tables(first, frequency[...], cosine.shape)
+
     own_gain = gain[:, pl.ds(pl.multiple_of(row * depth, depth), depth)]
 
     def weigh(kind, step):
@@ -127,30 +141,35 @@
             pieces[way][j].wait_recv()
             if j + 2 < 7:
                 go(pieces[way][j + 2])
+            go(across(way, j, kind_here))
+
+    def cross(j):
+        for way in range(2):
+            across(way, j, 1 - kind_here).wait_recv()
 
     arrive(0)
     hops[0].wait_recv()
     blocks[0, 2] = go(remote(hop.at[0], tile_rows(0, 2), tile_send.at[0, 2], tile_recv.at[0, 2], at(1, core)))
     hops[1].wait_recv()
     blocks[1, 2] = go(remote(hop.at[1], tile_rows(1, 2), tile_send.at[1, 2], tile_recv.at[1, 2], at(3, other)))
+    arrive(1)
     own_tile.wait()
     weigh(0, 0)
     blocks[1, 0].wait_recv()
     weigh(1, 0)
-    arrive(1)
+    arrive(2)
     for slot in (1, 3):
         blocks[0, slot].wait_recv()
         weigh(0, slot)
-    arrive(2)
+    arrive(3)
+    arrive(4)
     for slot in (1, 3):
         blocks[1, slot].wait_recv()
         weigh(1, slot)
-    arrive(3)
     for kind in (1, 0):
         blocks[kind, 2].wait_recv()
         weigh(kind, 2)
-    own_key.wait()
-    own_value.wait()
+    arrive(5)
 
     pairs, fars, nears = {}, {}, {}
 
@@ -200,14 +219,12 @@
 
     count = len(UNITS)
     for step in range(count + 3):
-        if step == 5:
-            arrive(5)
-        if step == 7:
+        if step == 1:
             arrive(6)
+        for j in {1: (0, 1), 3: (2, 3), 5: (4, 5), 7: (6,)}.get(step, ()):
+            cross(j)
         if step < count:
             multiply(step)
-        if step == 2:
-            arrive(4)
         if 0 <= step - 1 < count:
             relay(step - 1)
         if 0 <= step - 2 < count:
@@ -222,8 +239,8 @@
     rows, model = tokens.shape
     depth, width = w_key.shape
     pair = 2 * width
-    first = (lax.axis_index("row") * lax.axis_size("col") + lax.axis_index("col")) * rows
-    cosine, sine = rotation_tables(first + jnp.arange(rows, dtype=jnp.int32))
+    half_lane = np.arange(HEAD) % (HEAD // 2)
+    frequency = jnp.asarray(rope_base ** (-2.0 * half_lane / HEAD), jnp.float32).reshape(1, HEAD)
     units = len(UNITS)
     bf16, f32 = jnp.bfloat16, jnp.float32
     dma = pltpu.SemaphoreType.DMA
@@ -234,7 +251,7 @@
         kernel,
         name="key_value",
         out_shape=(out, out),
-        in_specs=[anywhere, vmem, anywhere, anywhere, vmem, vmem],
+        in_specs=[anywhere, vmem, anywhere, anywhere, vmem],
         out_specs=(vmem, vmem),
         scratch_shapes=[
             pltpu.VMEM((rows, model), bf16),
@@ -249,7 +266,10 @@
             pltpu.VMEM((units, 2, rows, pair), bf16),
             pltpu.VMEM((units, 2, rows, pair), bf16),
             pltpu.VMEM((rows, width), f32),
+            pltpu.VMEM((rows, width), f32),
+            pltpu.VMEM((rows, width), f32),
             dma((4,)),
+            dma((2, 7)), dma((2, 7)),
             dma((2, 7)), dma((2, 7)),
             dma((2,)), dma((2,)),
             dma((2, 4)), dma((2, 4)),
@@ -258,7 +278,7 @@
             dma((units, 2)), dma((units, 2)),
         ],
         compiler_params=pltpu.CompilerParams(collective_id=0, has_side_effects=True),
-    )(tokens, norm_gain.reshape(1, model), w_key, w_value, cosine, sine)
+    )(tokens, norm_gain.reshape(1, model), w_key, w_value, frequency)
 
 
 def solution(mesh):

time: 76.1 us -> 73.4 us (0.965)
  Pallas kernels: 69.8 us -> 68.3 us
  other arithmetic: 1.08 us -> 0 us
    pallas_call x1, Pallas kernels: 69.8 us -> 68.3 us  [body(): pl.pallas_call(kernel, name='key_value', out_shape=(out, out), in_specs=[...]
where the time goes in v2:
time: 73.4 us; the launch traced here: 72.3 us
  Pallas kernels  68.3 us (93%)
  local copies, waits for them, and re-layouts  3.34 us (5%)
    pallas_call x1, Pallas kernels, body(): pl.pallas_call(kernel, name='key_value', out_shape=(out, out), in_specs=[...  68.3 us
    unnamed x2, local copies, waits for them, and re-layouts  3.34 us

profile of v2, /device:TPU:1, one launch (start us, length us, event | category | flops | bytes accessed | tf_op | source)
XLA Modules:
  0.0 72.3 jit_solution(8148641904204893415)
XLA Ops:
  0.6 68.3 %key_value.1 = (bf16[128,1024]{1,0:T(8,128)(2,1)}, bf16[128,1024]{1,0:T(8,128)(2,1)}) custom-call(bf16[128,8192]{1,0:T(8,128)(2,1)} %tokens.1, f32[1,8192]{1,0:T(1,128)} %bitcast.1, bf16[1024,128]{1,0:T(8,128)(2,1)} %w_key.1, bf16[1024,128]{1,0:T(8,128)(2,1)} %w_value.1, f32[1,128]{1,0:T(1,128)} %constant.4.frequency), custom_call_target="tpu_custom_call" | custom-call | tf_op jit(solution)/shard_map/key_value/pallas_call | solution.py:250
  68.9 1.7 %copy.9 = bf16[128,1024]{1,0:T(8,128)(2,1)} copy(bf16[128,1024]{1,0:T(8,128)(2,1)} %get-tuple-element.4) | data formatting | bytes 524288
  70.6 1.7 %copy.10 = bf16[128,1024]{1,0:T(8,128)(2,1)} copy(bf16[128,1024]{1,0:T(8,128)(2,1)} %get-tuple-element.5) | data formatting | bytes 524288

commit v3 on v2

--- a/solution.py
+++ b/solution.py
@@ -25,7 +25,7 @@
 
 def kernel(
     tokens, gain, w_key, w_value, frequency, key_out, value_out,
-    tok, tile, weights, hop, kept, pair_out, pair_in, far_out, far_in, near_out, near_in, scale, cosine, sine,
+    tok, tile, weights, hop, kept, pair_out, pair_in, far_out, far_in, near_out, near_in, scale, cosine, sine, own_gain, own_frequency,
     local_sem, z_send, z_recv, x_send, x_recv, hop_send, hop_recv, tile_send, tile_recv,
     pair_send, pair_recv, far_send, far_recv, near_send, near_recv,
 ):
@@ -59,7 +59,11 @@
     own_value = pltpu.make_async_copy(w_value, weights.at[0, :, pl.ds(width, width)], local_sem.at[2])
     own_tile = pltpu.make_async_copy(features(0, core), tile_rows(0, 0), local_sem.at[0])
     own_tokens = pltpu.make_async_copy(tokens, tok, local_sem.at[3])
-    for copy in (own_key, own_value, own_tile, own_tokens):
+    gains = pltpu.make_async_copy(
+        gain.at[:, pl.ds(pl.multiple_of(row * depth, depth), depth)], own_gain, local_sem.at[4]
+    )
+    frequencies = pltpu.make_async_copy(frequency, own_frequency, local_sem.at[5])
+    for copy in (own_key, own_value, own_tile, own_tokens, gains, frequencies):
         copy.start()
 
     barrier = pltpu.get_barrier_semaphore()
@@ -127,14 +131,14 @@
     mean = jnp.sum(total, axis=1, keepdims=True) / tokens.shape[1]
     scale[...] = jnp.broadcast_to(lax.rsqrt(mean + EPS), scale.shape)
 
+    frequencies.wait()
+    gains.wait()
     first = (row * 8 + col) * rows
-    cosine[...], sine[...] = rotation_tables(first, frequency[...], cosine.shape)
-
-    own_gain = gain[:, pl.ds(pl.multiple_of(row * depth, depth), depth)]
+    cosine[...], sine[...] = rotation_tables(first, own_frequency[...], cosine.shape)
 
     def weigh(kind, step):
         ref = tile_rows(kind, step)
-        ref[...] = (ref[...].astype(jnp.float32) * own_gain).astype(jnp.bfloat16)
+        ref[...] = (ref[...].astype(jnp.float32) * own_gain[...]).astype(jnp.bfloat16)
 
     def arrive(j):
         for way in range(2):
@@ -218,19 +222,16 @@
         value_out[:, columns] = value.astype(jnp.bfloat16)
 
     count = len(UNITS)
-    for step in range(count + 3):
+    for step in range(count + 5):
         if step == 1:
             arrive(6)
         for j in {1: (0, 1), 3: (2, 3), 5: (4, 5), 7: (6,)}.get(step, ()):
             cross(j)
         if step < count:
             multiply(step)
-        if 0 <= step - 1 < count:
-            relay(step - 1)
-        if 0 <= step - 2 < count:
-            neighbour(step - 2)
-        if 0 <= step - 3 < count:
-            finish(step - 3)
+        for stage, lag in ((relay, 1), (neighbour, 3), (finish, 5)):
+            if 0 <= step - lag < count:
+                stage(step - lag)
     for copy in sent:
         copy.wait_send()
 
@@ -246,12 +247,12 @@
     dma = pltpu.SemaphoreType.DMA
     anywhere = pl.BlockSpec(memory_space=pl.ANY)
     vmem = pl.BlockSpec(memory_space=pltpu.VMEM)
-    out = jax.ShapeDtypeStruct((rows, units * width), bf16)
+    out = pltpu.VMEM((rows, units * width), bf16)
     return pl.pallas_call(
         kernel,
         name="key_value",
         out_shape=(out, out),
-        in_specs=[anywhere, vmem, anywhere, anywhere, vmem],
+        in_specs=[anywhere] * 5,
         out_specs=(vmem, vmem),
         scratch_shapes=[
             pltpu.VMEM((rows, model), bf16),
@@ -268,7 +269,9 @@
             pltpu.VMEM((rows, width), f32),
             pltpu.VMEM((rows, width), f32),
             pltpu.VMEM((rows, width), f32),
-            dma((4,)),
+            pltpu.VMEM((1, depth), f32),
+            pltpu.VMEM((1, width), f32),
+            dma((6,)),
             dma((2, 7)), dma((2, 7)),
             dma((2, 7)), dma((2, 7)),
             dma((2,)), dma((2,)),

time: 73.4 us -> 63.8 us (0.87); the launches traced: 72.3 us -> 63.7 us
  Pallas kernels: 68.3 us -> 61.6 us
  local copies, waits for them, and re-layouts: 3.34 us -> 1.41 us
    pallas_call x1, Pallas kernels: 68.3 us -> 61.6 us  [body(): pl.pallas_call(kernel, name='key_value', out_shape=(out, out), in_specs=[...]
    unnamed x2, local copies, waits for them, and re-layouts: 3.34 us -> 1.41 us
where the time goes in v3:
time: 63.8 us; the launch traced here: 63.7 us
  Pallas kernels  61.6 us (97%)
  local copies, waits for them, and re-layouts  1.41 us (2%)
  between operations  0.64 us (1%)
    pallas_call x1, Pallas kernels, body(): pl.pallas_call(kernel, name='key_value', out_shape=(out, out), in_specs=[...  61.6 us
    unnamed x2, local copies, waits for them, and re-layouts  1.41 us

profile of v3, /device:TPU:1, one launch (start us, length us, event | category | flops | bytes accessed | tf_op | source)
XLA Modules:
  0.0 63.7 jit_solution(2680594089051199452)
XLA Ops:
  0.6 61.6 %key_value.1 = (bf16[128,1024]{1,0:T(8,128)(2,1)S(1)}, bf16[128,1024]{1,0:T(8,128)(2,1)S(1)}) custom-call(bf16[128,8192]{1,0:T(8,128)(2,1)} %tokens.1, f32[1,8192]{1,0:T(1,128)} %bitcast.1, bf16[1024,128]{1,0:T(8,128)(2,1)} %w_key.1, bf16[1024,128]{1,0:T(8,128)(2,1)} %w_value.1, f32[1,128]{1,0:T(1,128)} %constant.4.frequency), custom_call_target="tpu_custom_call" | custom-call | tf_op jit(solution)/shard_map/key_value/pallas_call | solution.py:251
  62.3 0.7 %copy.9 = bf16[128,1024]{1,0:T(8,128)(2,1)} copy(bf16[128,1024]{1,0:T(8,128)(2,1)S(1)} %get-tuple-element.2) | data formatting | bytes 524288
  63.0 0.7 %copy.10 = bf16[128,1024]{1,0:T(8,128)(2,1)} copy(bf16[128,1024]{1,0:T(8,128)(2,1)S(1)} %get-tuple-element.3) | data formatting | bytes 524288

commit v4 on v3

--- a/solution.py
+++ b/solution.py
@@ -13,6 +13,7 @@
 rope_base = 500000.0
 
 UNITS = (0, 1, 7, 2, 6, 3, 5, 4)
+EARLY = 3
 
 
 def rotation_tables(first, frequency, shape):
@@ -114,13 +115,19 @@
         go(remote(features(2, other), hop.at[1], hop_send.at[1], hop_recv.at[1], at(3, core))),
     ]
     blocks = {}
-    for kind, step in ((0, 1), (0, 3), (1, 1), (1, 3), (1, 0)):
+
+    def block(kind, step):
         which = other if kind else core
         slot = (4 - step) % 4
         blocks[kind, slot] = go(
             remote(features(step, which), tile_rows(kind, slot), tile_send.at[kind, slot], tile_recv.at[kind, slot], at(step, which))
         )
 
+    for step in (1, 3):
+        block(0, step)
+    block(1, 0)
+
+
     own_tokens.wait()
 
     def squares(i, total):
@@ -130,11 +137,6 @@
     total = lax.fori_loop(0, tokens.shape[1] // 128, squares, jnp.zeros((rows, 128), jnp.float32))
     mean = jnp.sum(total, axis=1, keepdims=True) / tokens.shape[1]
     scale[...] = jnp.broadcast_to(lax.rsqrt(mean + EPS), scale.shape)
-
-    frequencies.wait()
-    gains.wait()
-    first = (row * 8 + col) * rows
-    cosine[...], sine[...] = rotation_tables(first, own_frequency[...], cosine.shape)
 
     def weigh(kind, step):
         ref = tile_rows(kind, step)
@@ -156,7 +158,10 @@
     blocks[0, 2] = go(remote(hop.at[0], tile_rows(0, 2), tile_send.at[0, 2], tile_recv.at[0, 2], at(1, core)))
     hops[1].wait_recv()
     blocks[1, 2] = go(remote(hop.at[1], tile_rows(1, 2), tile_send.at[1, 2], tile_recv.at[1, 2], at(3, other)))
+    for step in (1, 3):
+        block(1, step)
     arrive(1)
+    gains.wait()
     own_tile.wait()
     weigh(0, 0)
     blocks[1, 0].wait_recv()
@@ -167,15 +172,14 @@
         weigh(0, slot)
     arrive(3)
     arrive(4)
-    for slot in (1, 3):
-        blocks[1, slot].wait_recv()
-        weigh(1, slot)
-    for kind in (1, 0):
+    for kind in (0, 1):
         blocks[kind, 2].wait_recv()
         weigh(kind, 2)
-    arrive(5)
 
     pairs, fars, nears = {}, {}, {}
+
+    def keep(u):
+        kept[u] = jnp.dot(tile[pl.ds(0, 4 * rows), :], weights[UNITS[u]], preferred_element_type=jnp.float32)
 
     def multiply(u):
         w = weights[UNITS[u]]
@@ -183,7 +187,8 @@
             tile[pl.ds(4 * rows, 4 * rows), :], w, preferred_element_type=jnp.float32
         ).astype(jnp.bfloat16)
         pairs[u] = go(remote(pair_out.at[u], pair_in.at[u], pair_send.at[u], pair_recv.at[u], at(0, other)))
-        kept[u] = jnp.dot(tile[pl.ds(0, 4 * rows), :], w, preferred_element_type=jnp.float32)
+        if u >= EARLY:
+            keep(u)
 
     def chip_sum(u, step, low, size):
         at_rows = pl.ds(step * rows + low, size)
@@ -221,14 +226,27 @@
         key_out[:, columns] = turned.astype(jnp.bfloat16)
         value_out[:, columns] = value.astype(jnp.bfloat16)
 
+    keep(0)
+    for j in (0, 1):
+        cross(j)
+    for u in range(1, EARLY):
+        keep(u)
+    for slot in (1, 3):
+        blocks[1, slot].wait_recv()
+        weigh(1, slot)
+
     count = len(UNITS)
     for step in range(count + 5):
-        if step == 1:
-            arrive(6)
-        for j in {1: (0, 1), 3: (2, 3), 5: (4, 5), 7: (6,)}.get(step, ()):
+        for j in {1: (5,), 2: (6,)}.get(step, ()):
+            arrive(j)
+        for j in {3: (2, 3), 5: (4, 5), 7: (6,)}.get(step, ()):
             cross(j)
         if step < count:
             multiply(step)
+        if step == 3:
+            frequencies.wait()
+            first = (row * 8 + col) * rows
+            cosine[...], sine[...] = rotation_tables(first, own_frequency[...], cosine.shape)
         for stage, lag in ((relay, 1), (neighbour, 3), (finish, 5)):
             if 0 <= step - lag < count:
                 stage(step - lag)

time: 63.8 us -> 62.5 us (0.980)
  Pallas kernels: 61.6 us -> 60.3 us
    pallas_call x1, Pallas kernels: 61.6 us -> 60.3 us  [body(): pl.pallas_call(kernel, name='key_value', out_shape=(out, out), in_specs=[...]
where the time goes in v4:
time: 62.5 us; the launch traced here: 62.3 us
  Pallas kernels  60.3 us (96%)
  local copies, waits for them, and re-layouts  1.41 us (2%)
  between operations  0.64 us (1%)
    pallas_call x1, Pallas kernels, body(): pl.pallas_call(kernel, name='key_value', out_shape=(out, out), in_specs=[...  60.3 us
    unnamed x2, local copies, waits for them, and re-layouts  1.41 us

profile of v4, /device:TPU:1, one launch (start us, length us, event | category | flops | bytes accessed | tf_op | source)
XLA Modules:
  0.0 62.3 jit_solution(16619438990406363716)
XLA Ops:
  0.6 60.3 %key_value.1 = (bf16[128,1024]{1,0:T(8,128)(2,1)S(1)}, bf16[128,1024]{1,0:T(8,128)(2,1)S(1)}) custom-call(bf16[128,8192]{1,0:T(8,128)(2,1)} %tokens.1, f32[1,8192]{1,0:T(1,128)} %bitcast.1, bf16[1024,128]{1,0:T(8,128)(2,1)} %w_key.1, bf16[1024,128]{1,0:T(8,128)(2,1)} %w_value.1, f32[1,128]{1,0:T(1,128)} %constant.4.frequency), custom_call_target="tpu_custom_call" | custom-call | tf_op jit(solution)/shard_map/key_value/pallas_call | solution.py:269
  60.9 0.7 %copy.9 = bf16[128,1024]{1,0:T(8,128)(2,1)} copy(bf16[128,1024]{1,0:T(8,128)(2,1)S(1)} %get-tuple-element.2) | data formatting | bytes 524288
  61.6 0.7 %copy.10 = bf16[128,1024]{1,0:T(8,128)(2,1)} copy(bf16[128,1024]{1,0:T(8,128)(2,1)S(1)} %get-tuple-element.3) | data formatting | bytes 524288

commit v5 on v4

--- a/solution.py
+++ b/solution.py
@@ -127,16 +127,6 @@
         block(0, step)
     block(1, 0)
 
-
-    own_tokens.wait()
-
-    def squares(i, total):
-        part = tok[:, pl.ds(pl.multiple_of(i * 128, 128), 128)].astype(jnp.float32)
-        return total + part * part
-
-    total = lax.fori_loop(0, tokens.shape[1] // 128, squares, jnp.zeros((rows, 128), jnp.float32))
-    mean = jnp.sum(total, axis=1, keepdims=True) / tokens.shape[1]
-    scale[...] = jnp.broadcast_to(lax.rsqrt(mean + EPS), scale.shape)
 
     def weigh(kind, step):
         ref = tile_rows(kind, step)
@@ -235,6 +225,17 @@
         blocks[1, slot].wait_recv()
         weigh(1, slot)
 
+    def prepare_scale():
+        own_tokens.wait()
+
+        def squares(i, total):
+            part = tok[:, pl.ds(pl.multiple_of(i * 128, 128), 128)].astype(jnp.float32)
+            return total + part * part
+
+        total = lax.fori_loop(0, tokens.shape[1] // 128, squares, jnp.zeros((rows, 128), jnp.float32))
+        mean = jnp.sum(total, axis=1, keepdims=True) / tokens.shape[1]
+        scale[...] = jnp.broadcast_to(lax.rsqrt(mean + EPS), scale.shape)
+
     count = len(UNITS)
     for step in range(count + 5):
         for j in {1: (5,), 2: (6,)}.get(step, ()):
@@ -244,6 +245,7 @@
         if step < count:
             multiply(step)
         if step == 3:
+            prepare_scale()
             frequencies.wait()
             first = (row * 8 + col) * rows
             cosine[...], sine[...] = rotation_tables(first, own_frequency[...], cosine.shape)

time: 62.5 us -> 63 us (level)
  no operation moved by 1% of the time
where the time goes in v5:
time: 63 us; the launch traced here: 62.9 us
  Pallas kernels  60.8 us (97%)
  local copies, waits for them, and re-layouts  1.41 us (2%)
  between operations  0.64 us (1%)
    pallas_call x1, Pallas kernels, body(): pl.pallas_call(kernel, name='key_value', out_shape=(out, out), in_specs=[...  60.8 us
    unnamed x2, local copies, waits for them, and re-layouts  1.41 us

profile of v5, /device:TPU:1, one launch (start us, length us, event | category | flops | bytes accessed | tf_op | source)
XLA Modules:
  0.0 62.9 jit_solution(13967625396673553962)
XLA Ops:
  0.6 60.8 %key_value.1 = (bf16[128,1024]{1,0:T(8,128)(2,1)S(1)}, bf16[128,1024]{1,0:T(8,128)(2,1)S(1)}) custom-call(bf16[128,8192]{1,0:T(8,128)(2,1)} %tokens.1, f32[1,8192]{1,0:T(1,128)} %bitcast.1, bf16[1024,128]{1,0:T(8,128)(2,1)} %w_key.1, bf16[1024,128]{1,0:T(8,128)(2,1)} %w_value.1, f32[1,128]{1,0:T(1,128)} %constant.4.frequency), custom_call_target="tpu_custom_call" | custom-call | tf_op jit(solution)/shard_map/key_value/pallas_call | solution.py:271
  61.5 0.7 %copy.9 = bf16[128,1024]{1,0:T(8,128)(2,1)} copy(bf16[128,1024]{1,0:T(8,128)(2,1)S(1)} %get-tuple-element.2) | data formatting | bytes 524288
  62.2 0.7 %copy.10 = bf16[128,1024]{1,0:T(8,128)(2,1)} copy(bf16[128,1024]{1,0:T(8,128)(2,1)S(1)} %get-tuple-element.3) | data formatting | bytes 524288
